TPU v7x, 256 devices: a whole 4x4x8 slice. The times are simulated.
256 devices in a mesh: side: 2 (over x_lo), grp: 8 (over z), blk: 16 (over y, x_hi, core).
Axes of the slice: x: 4 (x_hi: 2, x_lo: 2; x = x_hi * 2 + x_lo), y: 4, z: 8, core: 2. Of those that a mesh axis runs over, the one named last changes fastest.
Arguments:
- embed_codes: bfloat16 [2, 65536, 128], P('side', ('grp', 'blk')), may hold values from -4 to 4
- embed_exps: int32 [2, 512], P('side', ('grp', 'blk')), may hold values from -1 to 1
- degrees: int32 [2, 65536], P('side', ('grp', 'blk')), may hold values from 16 to 128
- adjacency: bfloat16 [2, 49152, 128, 128], P('side', ('grp', 'blk')), may hold values from 0 to 1
- block_index: int32 [2, 2, 49152], P('side', None, ('grp', 'blk')), may hold values from 0 to 64, as said below
Outputs:
- layer_rows: bfloat16 [2, 65536, 128], P('side', ('grp', 'blk'))
Inputs may be any that keep to these rules, and one draw needn't show every extreme that they name: `block_index`: each device's list of 384 slots: its used slots come first, in non-decreasing source tile (row 1 below 64), with distinct (destination, source) pairs and destination tiles below 32; the remaining slots have source 64 and destination 0. Every list uses 384 // 4 slots or more, and in each section one list uses all 384.
All inputs are finite; a program needn't handle non-finite values.
Results may differ from a plain program's by a relative error of at most 0.0048.
Values may be sent and summed in bfloat16 or wider, within the bound.
A program may use at most 128 MiB of HBM per device.

v0:
```python
import jax
import jax.numpy as jnp
from jax import lax
from jax.sharding import PartitionSpec as P


def swapped(value, axis, stride):
    mask = 2**stride
    pairs = [(source, source ^ mask) for source in range(lax.axis_size(axis))]
    return lax.ppermute(value, axis, pairs)


def scale_rows(codes_part, exps_part, degree_part, tile_rows):
    scale = jnp.repeat(jnp.exp2(exps_part.astype(jnp.float32)), tile_rows, axis=1)
    inverse = lax.rsqrt(degree_part.astype(jnp.float32))
    return (codes_part.astype(jnp.float32) * scale[..., None] * inverse[..., None]).astype(
        jnp.bfloat16
    )


def shards(embed_codes, embed_exps, degrees, adjacency, block_index):
    tile_rows = adjacency.shape[2]
    row_width = embed_codes.shape[2]
    row_count = embed_codes.shape[1]
    tiles_dev = row_count // tile_rows
    groups = lax.axis_size("grp")
    dest_tiles = groups * tiles_dev
    capacity = adjacency.shape[1]
    other_codes, other_exps, other_degrees = swapped((embed_codes, embed_exps, degrees), "side", 0)
    source = scale_rows(other_codes, other_exps, other_degrees, tile_rows)
    panels = source.reshape(tiles_dev, tile_rows, row_width)
    target_tile = block_index[0, 0]
    source_tile = block_index[0, 1]
    own_blocks = adjacency[0]
    starting = jnp.zeros((dest_tiles, tile_rows, row_width), jnp.float32)
    piece = lax.all_gather(panels, "blk", axis=0, tiled=True)
    start = jnp.int32(0)
    piece_tiles = piece.shape[0]
    window = min(piece_tiles * dest_tiles, capacity)
    range_begin = jnp.sum((source_tile < start).astype(jnp.int32))
    range_end = jnp.sum((source_tile < start + piece_tiles).astype(jnp.int32))
    window_start = jnp.minimum(range_begin, capacity - window)
    picked = window_start + jnp.arange(window, dtype=jnp.int32)
    active = (picked >= range_begin) & (picked < range_end)
    offset_tiles = source_tile
    offset_tiles = jnp.clip(offset_tiles, 0, piece_tiles - 1)
    chosen = jnp.take(piece, offset_tiles, axis=0)
    products = jnp.einsum("kij,kjw->kiw", own_blocks, chosen, preferred_element_type=jnp.float32)
    placed = jnp.where(active, target_tile, dest_tiles)
    running = starting.at[placed].add(products, mode="drop")
    summed = lax.psum_scatter(
        running.reshape(groups, row_count, row_width), "grp", scatter_dimension=0, tiled=True
    )
    inverse = lax.rsqrt(degrees.astype(jnp.float32))
    return (summed * inverse[..., None]).astype(jnp.bfloat16)


def solution(mesh):
    placed = (
        P("side", ("grp", "blk"), None),
        P("side", ("grp", "blk")),
        P("side", ("grp", "blk")),
        P("side", ("grp", "blk"), None, None),
        P("side", None, ("grp", "blk")),
    )
    return jax.shard_map(
        shards,
        mesh=mesh,
        in_specs=placed,
        out_specs=P("side", ("grp", "blk"), None),
        check_vma=False,
    )
```

profile of v0, /device:TPU:2, one launch (start us, length us, event | category | flops | bytes accessed | tf_op | source)
XLA Modules:
  0.0 231.5 jit_solution(15946448544255334482)
XLA Ops:
  6.5 0.0 all-gather.2.cloned.1.call-start
  6.5 2.2 collective-permute-start
  8.8 0.0 collective-permute-start.2
  8.8 2.0 collective-permute-start.1
  10.8 1.9 collective-permute-done.1
  12.7 0.1 broadcast_bitcast_fusion
  12.7 0.0 collective-permute-done.2
  12.8 0.0 collective-permute-done
  12.8 0.9 multiply_convert_fusion.1
  13.6 0.0 all-gather.2.cloned.1.call-update
  13.7 0.0 reduce-scatter.2.cloned.1.call-start
  13.7 1.4 clamp_reduce_fusion
  15.7 2.0 fusion.11
  17.7 50.3 %all-gather.2.cloned.1.call-done = bf16[64,128,128]{2,1,0:T(8,128)(2,1)} async-done(((bf16[4,128,128]{2,1,0:T(8,128)(2,1)}), bf16[64,128,128]{2,1,0:T(8,128)(2,1)}) %all-gather.2.cloned.1.call-update) | async-done | bytes 2097168 | tf_op jit(solution)/shard_map/all_gather | solution.py:36
  68.1 12.9 %gather_fusion = bf16[384,128,128]{2,1,0:T(8,128)(2,1)} fusion(bf16[64,128,128]{2,1,0:T(8,128)(2,1)} %all-gather.2.cloned.1.call-done, s32[1024]{0:T(1024)S(1)} %pad_clamp_fusion), kind=kCustom, calls=%fused_computation | custom fusion | bytes 25167360 | tf_op jit(solution)/shard_map/jit(_take)/gather | solution.py:47
  81.0 22.7 %fusion.4 = f32[384,128,128]{1,2,0:T(8,128)} fusion(bf16[1,384,128,128]{3,2,1,0:T(8,128)(2,1)} %param.8, bf16[384,128,128]{2,1,0:T(8,128)(2,1)} %gather_fusion, pred[384]{0:T(512)(128)(4,1)S(1)} %compare_and_fusion), kind=kOutput, calls=%fused_computation.6 | convolution fusion | flops 1616904192 | bytes 50332032 | tf_op jit(solution)/shard_map/kij,kjw->kiw/dot_general | solution.py:48
  103.6 24.7 %copy.10 = f32[384,128,128]{2,1,0:T(8,128)} copy(f32[384,128,128]{1,2,0:T(8,128)} %fusion.4) | data formatting | bytes 50331648 | tf_op jit(solution)/shard_map/kij,kjw->kiw/dot_general | solution.py:48
  128.3 0.2 broadcast_in_dim.25
  128.5 0.0 copy-start.1
  128.5 50.2 %scatter_fusion = f32[32,128,128]{2,1,0:T(8,128)S(1)} fusion(f32[32,128,128]{2,1,0:T(8,128)S(1)} %broadcast_in_dim.25, s32[384]{0:T(512)S(1)} %get-tuple-element.9, f32[384,128,128]{2,1,0:T(8,128)} %copy.10), kind=kCustom, calls=%fused_computation.1 | custom fusion | flops 6291456 | bytes 75499008 | tf_op jit(solution)/shard_map/scatter-add | solution.py:50
  178.7 0.0 copy-start
  178.7 1.3 copy-done
  180.1 0.0 reduce-scatter.2.cloned.1.call-update
  180.1 0.0 copy-done.1
  180.1 42.8 %reduce-scatter.2.cloned.1.call-done = f32[1,512,128]{2,1,0:T(8,128)} async-done(((f32[8,512,128]{2,1,0:T(8,128)}), f32[1,512,128]{2,1,0:T(8,128)}) %reduce-scatter.2.cloned.1.call-update) | async-done | bytes 262160 | tf_op jit(solution)/shard_map/reduce_scatter | solution.py:51
  222.9 1.7 multiply_convert_fusion
  (5 shorter events, 0.0 us)
Async XLA Ops:
  6.5 61.5 %all-gather.2.cloned.1.call-start = ((), (), s32[]{:S(2)}) async-start(), calls=%async_computation.1 | async-start | bytes 2228224 | tf_op jit(solution)/shard_map/all_gather | solution.py:36
  6.5 6.2 %collective-permute-start = (bf16[1,512,128]{2,1,0:T(8,128)(2,1)}, bf16[1,512,128]{2,1,0:T(8,128)(2,1)S(1)}, u32[]{:S(2)}, u32[]{:S(2)}) collective-permute-start(bf16[1,512,128]{2,1,0:T(8,128)(2,1)} %param.5), channel_id=1, source_target_pairs={{0,128},{128,0},{1,129},{129,1},{2,130},{130,2},{3,131},{131,3},{4... | collective-permute-start | bytes 393224 | tf_op jit(solution)/shard_map/ppermute | solution.py:10
  8.8 4.0 %collective-permute-start.2 = (s32[1,512]{1,0:T(1,128)}, s32[1,512]{1,0:T(1,128)S(1)}, u32[]{:S(2)}, u32[]{:S(2)}) collective-permute-start(s32[1,512]{1,0:T(1,128)} %param.7), channel_id=1, source_target_pairs={{0,128},{128,0},{1,129},{129,1},{2,130},{130,2},{3,131},{131,3},{4... | collective-permute-start | bytes 6152 | tf_op jit(solution)/shard_map/ppermute | solution.py:10
  8.8 3.9 %collective-permute-start.1 = (s32[1,4]{1,0:T(1,128)}, s32[1,4]{1,0:T(1,128)S(1)}, u32[]{:S(2)}, u32[]{:S(2)}) collective-permute-start(s32[1,4]{1,0:T(1,128)} %param.6), channel_id=1, source_target_pairs={{0,128},{128,0},{1,129},{129,1},{2,130},{130,2},{3,131},{131,3},{4... | collective-permute-start | bytes 56 | tf_op jit(solution)/shard_map/ppermute | solution.py:10
  13.7 209.3 %reduce-scatter.2.cloned.1.call-start = ((), (), s32[]{:S(2)}) async-start(), calls=%async_computation.2 | async-start | bytes 2359296 | tf_op jit(solution)/shard_map/reduce_scatter | solution.py:51
  128.5 51.6 %copy-start.1 = (s32[1,512]{1,0:T(1,128)S(1)}, s32[1,512]{1,0:T(1,128)}, u32[]{:S(2)}) copy-start(s32[1,512]{1,0:T(1,128)} %param.7) | copy-start | bytes 6148
  178.7 1.4 copy-start
Sparse Core Ops, SparseCore 0:
  13.8 54.2 all-gather.1
  180.2 42.6 reduce-scatter.1
where the time goes:
time: 233 us; the launch traced here: 232 us
  waiting for transfers between devices  95 us (41%)
  other arithmetic  56.2 us (24%)
  local copies, waits for them, and re-layouts  39.2 us (17%)
  matrix products  22.7 us (10%)
  between operations  14.1 us (6%)
  starting transfers between devices  4.31 us (2%)
    all_gather x1, waiting for transfers between devices, shards(): piece = lax.all_gather(panels, 'blk', axis=0, tiled=True)  50.3 us
    scatter-add x1, other arithmetic, shards(): running = starting.at[placed].add(products, mode='drop')  50.2 us
    reduce_scatter x1, waiting for transfers between devices, shards(): lax.psum_scatter(running.reshape(groups, row_count, row_width), 'grp', sc...  42.8 us
    dot_general x1, local copies, waits for them, and re-layouts, shards(): jnp.einsum('kij,kjw->kiw', own_blocks, chosen, preferred_element_type=jnp...  24.7 us
    dot_general x1, matrix products, shards(): jnp.einsum('kij,kjw->kiw', own_blocks, chosen, preferred_element_type=jnp...  22.7 us
    gather x1, local copies, waits for them, and re-layouts, shards(): chosen = jnp.take(piece, offset_tiles, axis=0)  12.9 us
  transfers between devices with their start and end apart: 5, of which 3 were waited for; matrix products, arithmetic and copies ran while one was open for 2% of the time, Pallas kernels for 0%

commit v1 on v0

v1 whole, which is shorter than its diff:
```python
import functools

import jax
import jax.numpy as jnp
from jax import lax
from jax.experimental import pallas as pl
from jax.experimental.pallas import tpu as pltpu
from jax.sharding import PartitionSpec as P

MESH = pl.DeviceIdType.MESH
TILE = 128
TPS = 4
ROWS = TILE * TPS
HALF = ROWS // 2
QUARTER = HALF // 2
NY, NH, NC = 4, 2, 2
GROUPS = 8
DST = 32
SLOTS = 384
ADJ_PIECES = 8
DGROUP = 8


def kernel(
    codes_ref, exps_ref, deg_ref, adj_ref, index_ref, out_ref,
    a_ref, s_ref, t_ref, own_ref, acc_ref, inv_ref, tblv_ref, tbl_ref,
    ring_out, ring_in,
    adj_sem, tbl_sem,
    xa_s, xa_r, xb_s, xb_r, ya_s, ya_r, yr_s, yr_r, t_s, t_r, tr_s, tr_r,
    sib_s, sib_r, ring_s, ring_r,
):
    side = lax.axis_index("side")
    grp = lax.axis_index("grp")
    blk = lax.axis_index("blk")
    y, h, c = blk // (NH * NC), (blk // NC) % NH, blk % NC
    other = 1 - side

    def at(yy, hh, cc):
        return (yy * NH + hh) * NC + cc

    yu, yd, yo = (y + 1) % NY, (y + NY - 1) % NY, (y + 2) % NY
    gu, gd = (grp + 1) % GROUPS, (grp + GROUPS - 1) % GROUPS
    hs = (h, 1 - h)
    to_x = [(other, grp, at(y, hh, c)) for hh in hs]
    to_y = [(side, grp, at(yu, h, c)), (side, grp, at(yd, h, c))]
    to_sib = (side, grp, at(y, h, 1 - c))
    to_z = [(side, gu, blk), (side, gd, blk)]

    adj_copies = []
    per = SLOTS // ADJ_PIECES
    for piece in range(ADJ_PIECES):
        cut = pl.ds(piece * per, per)
        copy = pltpu.make_async_copy(adj_ref.at[cut], a_ref.at[cut], adj_sem.at[piece])
        copy.start()
        adj_copies.append(copy)

    barrier = pltpu.get_barrier_semaphore()
    partners = [*to_x, *to_y, to_sib, *to_z]
    for target in partners:
        pl.semaphore_signal(barrier, inc=1, device_id=target, device_id_type=MESH)

    for tile in range(TPS):
        lanes = deg_ref[0:1, tile * TILE:(tile + 1) * TILE].astype(jnp.float32)
        inverse = jnp.transpose(jnp.broadcast_to(lax.rsqrt(lanes), (TILE, TILE)))
        inv_ref[pl.ds(tile * TILE, TILE), :] = inverse
        power = jnp.exp2(jnp.full((TILE, TILE), exps_ref[0, tile], jnp.int32).astype(jnp.float32))
        rows = codes_ref[0, pl.ds(tile * TILE, TILE), :].astype(jnp.float32)
        rows = (rows * power * inverse).astype(jnp.bfloat16)
        if tile < TPS // 2:
            own_ref[pl.ds(tile * TILE, TILE), :] = rows
        else:
            t_ref[y, pl.ds((tile - TPS // 2) * TILE, TILE), :] = rows

    pl.semaphore_wait(barrier, len(partners))

    sends = []

    def send(src, dst, ssem, rsem, target):
        copy = pltpu.make_async_remote_copy(
            src_ref=src, dst_ref=dst, send_sem=ssem, recv_sem=rsem,
            device_id=target, device_id_type=MESH,
        )
        copy.start()
        sends.append(copy)

    def wait_in(dst, rsem):
        pltpu.make_async_copy(dst, dst, rsem).wait()

    def a_rows(yy, hh, cc):
        return s_ref.at[at(yy, hh, cc), pl.ds(0, HALF)]

    def b_rows(yy, hh, cc):
        return s_ref.at[at(yy, hh, cc), pl.ds(HALF, HALF)]

    for i in range(2):
        send(own_ref, a_rows(y, h, c), xa_s.at[i], xa_r.at[i], to_x[i])
        send(t_ref.at[y], t_ref.at[y], t_s.at[i], t_r.at[i], to_y[i])
    for i in range(2):
        send(t_ref.at[y], b_rows(y, h, c), xb_s.at[0, i], xb_r.at[0, i], to_x[i])

    flat = (
        lax.broadcasted_iota(jnp.int32, (NY * NH * NC, TILE), 0) * TILE
        + lax.broadcasted_iota(jnp.int32, (NY * NH * NC, TILE), 1)
    )

    def note(step, table):
        for j in range(16):
            k = step * 16 + j
            place = index_ref[0, 1, k] * DST + index_ref[0, 0, k]
            table = jnp.where(flat == place, k, table)
        return table

    tblv_ref[...] = lax.fori_loop(0, SLOTS // 16, note, jnp.full(flat.shape, SLOTS, jnp.int32))
    tbl_copy = pltpu.make_async_copy(tblv_ref, tbl_ref, tbl_sem)
    tbl_copy.start()
    a_ref[SLOTS] = jnp.zeros((TILE, TILE), jnp.bfloat16)
    acc_ref[...] = jnp.zeros_like(acc_ref)

    def product(source):
        rows = s_ref[source]

        def some(step, carry):
            parts = []
            for j in range(DGROUP):
                d = step * DGROUP + j
                parts.append(jnp.concatenate(
                    [a_ref[tbl_ref[source, q * DST + d]] for q in range(TPS)], axis=1))
            left = jnp.concatenate(parts, axis=0)
            cut = pl.ds(step * (DGROUP * TILE), DGROUP * TILE)
            acc_ref[cut, :] += jnp.dot(left, rows, preferred_element_type=jnp.float32)
            return carry

        lax.fori_loop(0, DST // DGROUP, some, 0)

    ys = (y, yu, yd, yo)

    def hand(number, ref):
        send(ref, ref, sib_s.at[number], sib_r.at[number], to_sib)

    def sib_in(number):
        k = number % 8
        rows = a_rows if number < 8 else b_rows
        wait_in(rows(ys[k // 2], hs[k % 2], 1 - c), sib_r.at[number])

    for i in range(2):
        frm = yd if i == 0 else yu
        wait_in(t_ref.at[frm], t_r.at[i])
        quarter = t_ref.at[frm, pl.ds(i * QUARTER, QUARTER)]
        send(quarter, quarter, tr_s.at[i], tr_r.at[i], to_y[i])
    for i in range(2):
        ref = a_rows(y, hs[i], c)
        wait_in(ref, xa_r.at[i])
        for v in range(2):
            send(ref, ref, ya_s.at[v, i], ya_r.at[v, i], to_y[v])
        hand(i, ref)
    for n, frm in ((1, yu), (2, yd)):
        for i in range(2):
            send(t_ref.at[frm], b_rows(frm, h, c), xb_s.at[n, i], xb_r.at[n, i], to_x[i])
    tbl_copy.wait()
    for copy in adj_copies:
        copy.wait()
    for i in range(2):
        ref = b_rows(y, hs[i], c)
        wait_in(ref, xb_r.at[0, i])
        hand(8 + i, ref)
    for i in range(2):
        product(at(y, hs[i], c))
    for i in range(2):
        wait_in(t_ref.at[yo, pl.ds(i * QUARTER, QUARTER)], tr_r.at[i])
    for i in range(2):
        send(t_ref.at[yo], b_rows(yo, h, c), xb_s.at[3, i], xb_r.at[3, i], to_x[i])
    for i in range(2):
        sib_in(i)
        sib_in(8 + i)
        product(at(y, hs[i], 1 - c))
    for i in range(2):
        for v in range(2):
            frm = yd if v == 0 else yu
            ref = a_rows(frm, hs[i], c)
            wait_in(ref, ya_r.at[v, i])
            if i == v:
                send(ref, ref, yr_s.at[i], yr_r.at[i], to_y[v])
            hand((4 if v == 0 else 2) + i, ref)
    for n, frm in ((1, yu), (2, yd)):
        for i in range(2):
            ref = b_rows(frm, hs[i], c)
            wait_in(ref, xb_r.at[n, i])
            hand(8 + 2 * n + i, ref)
    for n, frm in ((1, yu), (2, yd)):
        for i in range(2):
            product(at(frm, hs[i], c))
    for i in range(2):
        ref = b_rows(yo, hs[i], c)
        wait_in(ref, xb_r.at[3, i])
        hand(14 + i, ref)
    for n, frm in ((1, yu), (2, yd)):
        for i in range(2):
            sib_in(2 * n + i)
            sib_in(8 + 2 * n + i)
            product(at(frm, hs[i], 1 - c))
    for i in range(2):
        ref = a_rows(yo, hs[i], c)
        wait_in(ref, yr_r.at[i])
        hand(6 + i, ref)
    for i in range(2):
        product(at(yo, hs[i], c))
    for i in range(2):
        sib_in(6 + i)
        sib_in(14 + i)
        product(at(yo, hs[i], 1 - c))

    for m in range(7):
        reach = 4 - (m + 1) // 2
        for way in range(2):
            part = (m % 2) ^ way
            dest = (grp + reach) % GROUPS if way == 0 else (grp + GROUPS - reach) % GROUPS
            value = acc_ref[pl.ds(dest * ROWS + part * HALF, HALF), :]
            if m >= 2:
                wait_in(ring_in.at[way, m - 2], ring_r.at[way, m - 2])
                value = value + ring_in[way, m - 2].astype(jnp.float32)
            ring_out[way, m] = value.astype(jnp.bfloat16)
            send(ring_out.at[way, m], ring_in.at[way, m], ring_s.at[way, m], ring_r.at[way, m], to_z[way])
    for way in range(2):
        wait_in(ring_in.at[way, 5], ring_r.at[way, 5])
    for way in range(2):
        wait_in(ring_in.at[way, 6], ring_r.at[way, 6])
    for part in range(2):
        value = acc_ref[pl.ds(grp * ROWS + part * HALF, HALF), :]
        value = value + ring_in[part, 6].astype(jnp.float32)
        value = value + ring_in[1 - part, 5].astype(jnp.float32)
        value = value * inv_ref[pl.ds(part * HALF, HALF), :]
        out_ref[0, pl.ds(part * HALF, HALF), :] = value.astype(jnp.bfloat16)
    for copy in sends:
        copy.wait_send()


def shards(embed_codes, embed_exps, degrees, adjacency, block_index):
    width = embed_codes.shape[2]
    dma = pltpu.SemaphoreType.DMA
    vmem = pl.BlockSpec(memory_space=pltpu.VMEM)
    smem = pl.BlockSpec(memory_space=pltpu.SMEM)
    return pl.pallas_call(
        kernel,
        out_shape=jax.ShapeDtypeStruct(embed_codes.shape, jnp.bfloat16),
        in_specs=[vmem, smem, vmem, pl.BlockSpec(memory_space=pl.ANY), smem],
        out_specs=vmem,
        scratch_shapes=[
            pltpu.VMEM((SLOTS + 1, TILE, TILE), jnp.bfloat16),
            pltpu.VMEM((NY * NH * NC, ROWS, width), jnp.bfloat16),
            pltpu.VMEM((NY, HALF, width), jnp.bfloat16),
            pltpu.VMEM((HALF, width), jnp.bfloat16),
            pltpu.VMEM((DST * TILE, width), jnp.float32),
            pltpu.VMEM((ROWS, width), jnp.float32),
            pltpu.VMEM((NY * NH * NC, TILE), jnp.int32),
            pltpu.SMEM((NY * NH * NC, TILE), jnp.int32),
            pltpu.VMEM((2, 7, HALF, width), jnp.bfloat16),
            pltpu.VMEM((2, 7, HALF, width), jnp.bfloat16),
            dma((ADJ_PIECES,)), dma(()),
            dma((2,)), dma((2,)), dma((4, 2)), dma((4, 2)), dma((2, 2)), dma((2, 2)),
            dma((2,)), dma((2,)), dma((2,)), dma((2,)), dma((2,)), dma((2,)),
            dma((16,)), dma((16,)), dma((2, 7)), dma((2, 7)),
        ],
        compiler_params=pltpu.CompilerParams(
            collective_id=0, has_side_effects=True, vmem_limit_bytes=48 * 2**20
        ),
    )(embed_codes, embed_exps, degrees, adjacency.reshape(adjacency.shape[1:]), block_index)


def solution(mesh):
    placed = (
        P("side", ("grp", "blk"), None),
        P("side", ("grp", "blk")),
        P("side", ("grp", "blk")),
        P("side", ("grp", "blk"), None, None),
        P("side", None, ("grp", "blk")),
    )
    return jax.shard_map(
        shards,
        mesh=mesh,
        in_specs=placed,
        out_specs=P("side", ("grp", "blk"), None),
        check_vma=False,
    )
```

time: 233 us -> 60.5 us (0.26)
  the two profiles are of different devices: /device:TPU:2 before, /device:TPU:32 now
where the time goes in v1:
time: 60.5 us; the launch traced here: 60.3 us
  Pallas kernels  56.7 us (94%)
  local copies, waits for them, and re-layouts  3.58 us (6%)
    pallas_call x1, Pallas kernels, shards(): pl.pallas_call(kernel, out_shape=jax.ShapeDtypeStruct(embed_codes.shape,...  56.7 us
    unnamed x9, local copies, waits for them, and re-layouts  3.58 us

profile of v1, /device:TPU:32, one launch (start us, length us, event | category | flops | bytes accessed | tf_op | source)
XLA Modules:
  0.0 60.3 jit_solution(15417492081204533137)
XLA Ops:
  0.0 0.0 copy-start
  0.0 0.9 %copy-done = bf16[1,512,128]{2,1,0:T(8,128)(2,1)S(1)} copy-done((bf16[1,512,128]{2,1,0:T(8,128)(2,1)S(1)}, bf16[1,512,128]{2,1,0:T(8,128)(2,1)}, u32[]{:S(2)}) %copy-start) | copy-done | bytes 131096
  0.9 0.0 copy-start.1
  0.9 0.7 %copy-done.1 = s32[1,2,384]{2,1,0:T(2,128)S(1)} copy-done((s32[1,2,384]{2,1,0:T(2,128)S(1)}, s32[1,2,384]{2,1,0:T(2,128)}, u32[]{:S(2)}) %copy-start.1) | copy-done | bytes 3096
  1.6 0.0 copy-start.2
  1.6 0.7 %copy-done.2 = s32[1,512]{1,0:T(1,128)S(1)} copy-done((s32[1,512]{1,0:T(1,128)S(1)}, s32[1,512]{1,0:T(1,128)}, u32[]{:S(2)}) %copy-start.2) | copy-done | bytes 2072
  2.3 0.0 copy-start.3
  2.3 0.7 %copy-done.3 = s32[1,4]{1,0:T(1,128)S(1)} copy-done((s32[1,4]{1,0:T(1,128)S(1)}, s32[1,4]{1,0:T(1,128)}, u32[]{:S(2)}) %copy-start.3) | copy-done | bytes 40
  2.9 56.7 %shard_map.55 = bf16[1,512,128]{2,1,0:T(8,128)(2,1)S(1)} custom-call(bf16[1,512,128]{2,1,0:T(8,128)(2,1)S(1)} %copy-done, s32[1,4]{1,0:T(1,128)S(1)} %copy-done.3, s32[1,512]{1,0:T(1,128)S(1)} %copy-done.2, bf16[384,128,128]{2,1,0:T(8,128)(2,1)} %bitcast.1, s32[1,2,384]{2,1,0:T(2,128)S(1)} %copy-done.1), custom_call_target="tpu_custom_call" | custom-call | tf_op jit(solution)/shard_map/pallas_call | solution.py:242
  59.7 0.7 %copy.7 = bf16[1,512,128]{2,1,0:T(8,128)(2,1)} copy(bf16[1,512,128]{2,1,0:T(8,128)(2,1)S(1)} %shard_map.55) | data formatting | bytes 262144
Async XLA Ops:
  0.0 0.9 %copy-start = (bf16[1,512,128]{2,1,0:T(8,128)(2,1)S(1)}, bf16[1,512,128]{2,1,0:T(8,128)(2,1)}, u32[]{:S(2)}) copy-start(bf16[1,512,128]{2,1,0:T(8,128)(2,1)} %codes_ref.1) | copy-start | bytes 393220
  0.9 0.7 %copy-start.1 = (s32[1,2,384]{2,1,0:T(2,128)S(1)}, s32[1,2,384]{2,1,0:T(2,128)}, u32[]{:S(2)}) copy-start(s32[1,2,384]{2,1,0:T(2,128)} %index_ref.1) | copy-start | bytes 9220
  1.6 0.7 %copy-start.2 = (s32[1,512]{1,0:T(1,128)S(1)}, s32[1,512]{1,0:T(1,128)}, u32[]{:S(2)}) copy-start(s32[1,512]{1,0:T(1,128)} %deg_ref.1) | copy-start | bytes 6148
  2.3 0.7 %copy-start.3 = (s32[1,4]{1,0:T(1,128)S(1)}, s32[1,4]{1,0:T(1,128)}, u32[]{:S(2)}) copy-start(s32[1,4]{1,0:T(1,128)} %exps_ref.1) | copy-start | bytes 52

commit v2 on v1

v2 whole, which is shorter than its diff:
```python
import functools

import jax
import jax.numpy as jnp
from jax import lax
from jax.experimental import pallas as pl
from jax.experimental.pallas import tpu as pltpu
from jax.sharding import PartitionSpec as P

MESH = pl.DeviceIdType.MESH
TILE = 128
TPS = 4
ROWS = TILE * TPS
HALF = ROWS // 2
NY, NH, NC = 4, 2, 2
GROUPS = 8
DST = 32
SLOTS = 384
ADJ_PIECES = 8
PAIRS = (SLOTS + DST) // 2
UNROLL = 8
NSRC = 64


def kernel(
    codes_hbm, exps_hbm, deg_hbm, adj_ref, index_hbm, out_ref,
    a_ref, s_ref, t_ref, own_ref, sum_ref, inv_ref, tblv_ref, tbl_ref,
    codes_ref, exps_ref, deg_ref, index_ref,
    ring_out, ring_in,
    in_sem, adj_sem, tbl_sem,
    xa_s, xa_r, xb_s, xb_r, ya_s, ya_r, yr_s, yr_r, t_s, t_r, tr_s, tr_r,
    sib_s, sib_r, ring_s, ring_r,
):
    side = lax.axis_index("side")
    grp = lax.axis_index("grp")
    blk = lax.axis_index("blk")
    y, h, c = blk // (NH * NC), (blk // NC) % NH, blk % NC
    other = 1 - side

    def at(yy, hh, cc):
        return (yy * NH + hh) * NC + cc

    yu, yd, yo = (y + 1) % NY, (y + NY - 1) % NY, (y + 2) % NY
    gu, gd = (grp + 1) % GROUPS, (grp + GROUPS - 1) % GROUPS
    hs = (h, 1 - h)
    to_x = [(other, grp, at(y, hh, c)) for hh in hs]
    to_y = [(side, grp, at(yu, h, c)), (side, grp, at(yd, h, c))]
    to_sib = (side, grp, at(y, h, 1 - c))
    to_z = [(side, gu, blk), (side, gd, blk)]

    barrier = pltpu.get_barrier_semaphore()
    partners = [*to_x, *to_y, to_sib, *to_z]
    for target in partners:
        pl.semaphore_signal(barrier, inc=1, device_id=target, device_id_type=MESH)

    small = [
        pltpu.make_async_copy(src, dst, in_sem.at[i])
        for i, (src, dst) in enumerate((
            (exps_hbm, exps_ref), (deg_hbm, deg_ref), (codes_hbm, codes_ref), (index_hbm, index_ref)))
    ]
    for copy in small:
        copy.start()
    adj_copies = []
    per = SLOTS // ADJ_PIECES
    for piece in range(ADJ_PIECES):
        cut = pl.ds(piece * per, per)
        copy = pltpu.make_async_copy(adj_ref.at[cut], a_ref.at[cut], adj_sem.at[piece])
        copy.start()
        adj_copies.append(copy)

    def column(row):
        return jnp.transpose(jnp.broadcast_to(row, (TILE, TILE)))

    for copy in small[:3]:
        copy.wait()
    for tile in range(TPS):
        lanes = deg_ref[0:1, tile * TILE:(tile + 1) * TILE].astype(jnp.float32)
        inverse = column(lax.rsqrt(lanes))
        inv_ref[pl.ds(tile * TILE, TILE), :] = inverse
        power = jnp.exp2(jnp.full((TILE, TILE), exps_ref[0, tile], jnp.int32).astype(jnp.float32))
        rows = codes_ref[0, pl.ds(tile * TILE, TILE), :].astype(jnp.float32)
        rows = (rows * power * inverse).astype(jnp.bfloat16)
        if tile < TPS // 2:
            own_ref[tile] = rows
        else:
            t_ref[y, tile - TPS // 2] = rows

    pl.semaphore_wait(barrier, len(partners))

    sends = []

    def send(src, dst, ssem, rsem, target):
        copy = pltpu.make_async_remote_copy(
            src_ref=src, dst_ref=dst, send_sem=ssem, recv_sem=rsem,
            device_id=target, device_id_type=MESH,
        )
        copy.start()
        sends.append(copy)

    def wait_in(dst, rsem):
        pltpu.make_async_copy(dst, dst, rsem).wait()

    def a_rows(yy, hh, cc):
        return s_ref.at[pl.ds(at(yy, hh, cc) * TPS, TPS // 2)]

    def b_rows(yy, hh, cc):
        return s_ref.at[pl.ds(at(yy, hh, cc) * TPS + TPS // 2, TPS // 2)]

    for i in range(2):
        send(own_ref, a_rows(y, h, c), xa_s.at[i], xa_r.at[i], to_x[i])
        send(t_ref.at[y], t_ref.at[y], t_s.at[i], t_r.at[i], to_y[i])
    for i in range(2):
        send(t_ref.at[y], b_rows(y, h, c), xb_s.at[0, i], xb_r.at[0, i], to_x[i])

    small[3].wait()
    sub = lax.broadcasted_iota(jnp.int32, (TILE, TILE), 0)
    lane = lax.broadcasted_iota(jnp.int32, (TILE, TILE), 1)
    lane_row = lax.broadcasted_iota(jnp.int32, (1, TILE), 1)
    cuts = range(SLOTS // TILE)

    def down(mask, value=1):
        return jnp.sum(jnp.where(mask, value, 0), axis=0, keepdims=True)

    target = [index_ref[0, 0:1, j * TILE:(j + 1) * TILE] for j in cuts]
    source = [index_ref[0, 1:2, j * TILE:(j + 1) * TILE] for j in cuts]
    used = [q < NSRC for q in source]
    key = [jnp.where(u, t, DST) for u, t in zip(used, target)]
    key_col = [column(t) for t in key]
    count = sum(down(k == lane) for k in key_col)
    padded = jnp.where(lane_row < DST, (count + 1) // 2 * 2, 0)
    padded_col = column(padded)
    begin = down(sub < lane, padded_col)
    begin_col = column(begin)
    place_col, code_col = [], []
    for j in cuts:
        rank = down((key_col[j] == key[j]) & (sub < lane))
        for i in range(j):
            rank = rank + down(key_col[i] == key[j])
        place = down(sub < key[j], padded_col) + rank
        place_col.append(column(jnp.where(used[j], place, 8 * TILE)))
        code_col.append(((j * TILE + sub) * NSRC + column(source[j])) * 2)
    for r in range(4):
        spot = lane + r * TILE
        code = jnp.full((TILE, TILE), -1, jnp.int32)
        for j in cuts:
            code = jnp.where(place_col[j] == spot, code_col[j], code)
        code = jnp.max(code, axis=0, keepdims=True)
        first = down((begin_col == spot) & (padded_col > 0))
        tblv_ref[r:r + 1, :] = jnp.where(code < 0, SLOTS * NSRC * 2, code) + first
    tblv_ref[4:5, :] = jnp.where(padded > 0, (begin + padded) // 2 - 1, PAIRS)
    tbl_copy = pltpu.make_async_copy(tblv_ref, tbl_ref, tbl_sem)
    tbl_copy.start()
    a_ref[SLOTS] = jnp.zeros((TILE, TILE), jnp.bfloat16)
    sum_ref[PAIRS] = jnp.zeros((TILE, TILE), jnp.float32)

    def products():
        def some(step, total):
            for j in range(UNROLL):
                pair = step * UNROLL + j
                row, spot = pair // (TILE // 2), pair % (TILE // 2) * 2
                one, two = tbl_ref[row, spot], tbl_ref[row, spot + 1]
                left = jnp.concatenate([a_ref[one // (2 * NSRC)], a_ref[two // (2 * NSRC)]], axis=1)
                right = jnp.concatenate(
                    [s_ref[one // 2 % NSRC], s_ref[two // 2 % NSRC]], axis=0)
                value = jnp.dot(left, right, preferred_element_type=jnp.float32)
                keep = (1 - one % 2).astype(jnp.float32)
                total = value + total * keep
                sum_ref[pair] = total
            return total

        lax.fori_loop(0, PAIRS // UNROLL, some, jnp.zeros((TILE, TILE), jnp.float32))

    def summed(group, part):
        at_tile = group * TPS + part * (TPS // 2)
        return jnp.concatenate(
            [sum_ref[tbl_ref[4, at_tile + j]] for j in range(TPS // 2)], axis=0)

    ys = (y, yu, yd, yo)

    def hand(number, ref):
        send(ref, ref, sib_s.at[number], sib_r.at[number], to_sib)

    def sib_in(number):
        k = number % 8
        rows = a_rows if number < 8 else b_rows
        wait_in(rows(ys[k // 2], hs[k % 2], 1 - c), sib_r.at[number])

    for i in range(2):
        frm = yd if i == 0 else yu
        wait_in(t_ref.at[frm], t_r.at[i])
        tile = t_ref.at[frm, i]
        send(tile, tile, tr_s.at[i], tr_r.at[i], to_y[i])
        for v in range(2):
            send(t_ref.at[frm], b_rows(frm, h, c), xb_s.at[2 - i, v], xb_r.at[2 - i, v], to_x[v])
    for i in range(2):
        ref = a_rows(y, hs[i], c)
        wait_in(ref, xa_r.at[i])
        for v in range(2):
            send(ref, ref, ya_s.at[v, i], ya_r.at[v, i], to_y[v])
        hand(i, ref)
    for i in range(2):
        ref = b_rows(y, hs[i], c)
        wait_in(ref, xb_r.at[0, i])
        hand(8 + i, ref)
    for i in range(2):
        wait_in(t_ref.at[yo, i], tr_r.at[i])
    for i in range(2):
        send(t_ref.at[yo], b_rows(yo, h, c), xb_s.at[3, i], xb_r.at[3, i], to_x[i])
    for i in range(2):
        for v in (i, 1 - i):
            frm = yd if v == 0 else yu
            ref = a_rows(frm, hs[i], c)
            wait_in(ref, ya_r.at[v, i])
            if i == v:
                send(ref, ref, yr_s.at[i], yr_r.at[i], to_y[v])
            hand((4 if v == 0 else 2) + i, ref)
    for n, frm in ((2, yd), (1, yu)):
        for i in range(2):
            ref = b_rows(frm, hs[i], c)
            wait_in(ref, xb_r.at[n, i])
            hand(8 + 2 * n + i, ref)
    for i in range(2):
        ref = b_rows(yo, hs[i], c)
        wait_in(ref, xb_r.at[3, i])
        hand(14 + i, ref)
    for i in range(2):
        ref = a_rows(yo, hs[i], c)
        wait_in(ref, yr_r.at[i])
        hand(6 + i, ref)
    tbl_copy.wait()
    for copy in adj_copies:
        copy.wait()
    for number in range(16):
        sib_in(number)
    products()

    for m in range(7):
        reach = 4 - (m + 1) // 2
        for way in range(2):
            part = (m % 2) ^ way
            dest = (grp + reach) % GROUPS if way == 0 else (grp + GROUPS - reach) % GROUPS
            value = summed(dest, part)
            if m >= 2:
                wait_in(ring_in.at[way, m - 2], ring_r.at[way, m - 2])
                value = value + ring_in[way, m - 2].astype(jnp.float32)
            ring_out[way, m] = value.astype(jnp.bfloat16)
            send(ring_out.at[way, m], ring_in.at[way, m], ring_s.at[way, m], ring_r.at[way, m], to_z[way])
    for way in range(2):
        wait_in(ring_in.at[way, 5], ring_r.at[way, 5])
    for way in range(2):
        wait_in(ring_in.at[way, 6], ring_r.at[way, 6])
    for part in range(2):
        value = summed(grp, part)
        value = value + ring_in[part, 6].astype(jnp.float32)
        value = value + ring_in[1 - part, 5].astype(jnp.float32)
        value = value * inv_ref[pl.ds(part * HALF, HALF), :]
        out_ref[0, pl.ds(part * HALF, HALF), :] = value.astype(jnp.bfloat16)
    for copy in sends:
        copy.wait_send()


def shards(embed_codes, embed_exps, degrees, adjacency, block_index):
    width = embed_codes.shape[2]
    dma = pltpu.SemaphoreType.DMA
    vmem = pl.BlockSpec(memory_space=pltpu.VMEM)
    return pl.pallas_call(
        kernel,
        out_shape=jax.ShapeDtypeStruct(embed_codes.shape, jnp.bfloat16),
        in_specs=[pl.BlockSpec(memory_space=pltpu.HBM)] * 5,
        out_specs=vmem,
        scratch_shapes=[
            pltpu.VMEM((SLOTS + 1, TILE, TILE), jnp.bfloat16),
            pltpu.VMEM((NSRC, TILE, width), jnp.bfloat16),
            pltpu.VMEM((NY, TPS // 2, TILE, width), jnp.bfloat16),
            pltpu.VMEM((TPS // 2, TILE, width), jnp.bfloat16),
            pltpu.VMEM((PAIRS + 1, TILE, width), jnp.float32),
            pltpu.VMEM((ROWS, width), jnp.float32),
            pltpu.VMEM((8, TILE), jnp.int32),
            pltpu.SMEM((8, TILE), jnp.int32),
            pltpu.VMEM(embed_codes.shape, embed_codes.dtype),
            pltpu.SMEM(embed_exps.shape, embed_exps.dtype),
            pltpu.VMEM(degrees.shape, degrees.dtype),
            pltpu.VMEM(block_index.shape, block_index.dtype),
            pltpu.VMEM((2, 7, HALF, width), jnp.bfloat16),
            pltpu.VMEM((2, 7, HALF, width), jnp.bfloat16),
            dma((4,)), dma((ADJ_PIECES,)), dma(()),
            dma((2,)), dma((2,)), dma((4, 2)), dma((4, 2)), dma((2, 2)), dma((2, 2)),
            dma((2,)), dma((2,)), dma((2,)), dma((2,)), dma((2,)), dma((2,)),
            dma((16,)), dma((16,)), dma((2, 7)), dma((2, 7)),
        ],
        compiler_params=pltpu.CompilerParams(
            collective_id=0, has_side_effects=True, vmem_limit_bytes=67_043_328
        ),
    )(embed_codes, embed_exps, degrees, adjacency.reshape(adjacency.shape[1:]), block_index)


def solution(mesh):
    placed = (
        P("side", ("grp", "blk"), None),
        P("side", ("grp", "blk")),
        P("side", ("grp", "blk")),
        P("side", ("grp", "blk"), None, None),
        P("side", None, ("grp", "blk")),
    )
    return jax.shard_map(
        shards,
        mesh=mesh,
        in_specs=placed,
        out_specs=P("side", ("grp", "blk"), None),
        check_vma=False,
    )
```

time: 60.5 us -> 50.5 us (0.83)
  the two profiles are of different devices: /device:TPU:32 before, /device:TPU:1 now
where the time goes in v2:
time: 50.5 us; the launch traced here: 50.4 us
  Pallas kernels  48.8 us (97%)
  local copies, waits for them, and re-layouts  1.57 us (3%)
    pallas_call x1, Pallas kernels, shards(): pl.pallas_call(kernel, out_shape=jax.ShapeDtypeStruct(embed_codes.shape,...  48.8 us
    unnamed x1, local copies, waits for them, and re-layouts  1.57 us

profile of v2, /device:TPU:1, one launch (start us, length us, event | category | flops | bytes accessed | tf_op | source)
XLA Modules:
  0.0 50.4 jit_solution(8351032645549142325)
XLA Ops:
  0.0 48.8 %shard_map.55 = bf16[1,512,128]{2,1,0:T(8,128)(2,1)} custom-call(bf16[1,512,128]{2,1,0:T(8,128)(2,1)} %codes_hbm.1, s32[1,4]{1,0:T(1,128)} %exps_hbm.1, s32[1,512]{1,0:T(1,128)} %deg_hbm.1, bf16[384,128,128]{2,1,0:T(8,128)(2,1)} %bitcast.1, s32[1,2,384]{2,1,0:T(2,128)} %index_hbm.1), custom_call_target="tpu_custom_call" | custom-call | tf_op jit(solution)/shard_map/pallas_call | solution.py:266
  48.9 1.6 %copy.7 = bf16[1,512,128]{2,1,0:T(8,128)(2,1)} copy(bf16[1,512,128]{2,1,0:T(8,128)(2,1)} %shard_map.55) | data formatting | bytes 262144

commit v3 on v2

v3 whole, which is shorter than its diff:
```python
import jax
import jax.numpy as jnp
from jax import lax
from jax.experimental import pallas as pl
from jax.experimental.pallas import tpu as pltpu
from jax.sharding import PartitionSpec as P

MESH = pl.DeviceIdType.MESH
TILE = 128
TPS = 4
PART = TPS // 2
FEATS = TILE // 2
NY, NH, NC = 4, 2, 2
GROUPS = 8
DST = 32
SLOTS = 384
NSRC = 64
ADJ_PIECES = 8
PAIRS = (SLOTS + DST) // 2
SEGMENTS = ((0, 64, 32), (64, 64, 32), (128, 80, 40))


def kernel(
    codes_hbm, exps_hbm, deg_hbm, adj_ref, index_hbm, out_ref,
    a_ref, s0_ref, s1_ref, t_ref, own_ref, sum_ref, fin_ref, tblv_ref, tbl_ref,
    codes_ref, exps_ref, deg_ref, index_ref,
    ring_out, ring_in,
    in_sem, adj_sem, tbl_sem,
    xa_s, xa_r, xb_s, xb_r, ya_s, ya_r, yr_s, yr_r, t_s, t_r, tr_s, tr_r,
    sib_s, sib_r, ring_s, ring_r,
):
    s_refs = (s0_ref, s1_ref)
    side = lax.axis_index("side")
    grp = lax.axis_index("grp")
    blk = lax.axis_index("blk")
    y, h, c = blk // (NH * NC), (blk // NC) % NH, blk % NC
    other = 1 - side

    def at(yy, hh, cc):
        return (yy * NH + hh) * NC + cc

    yu, yd, yo = (y + 1) % NY, (y + NY - 1) % NY, (y + 2) % NY
    gu, gd = (grp + 1) % GROUPS, (grp + GROUPS - 1) % GROUPS
    hs = (h, 1 - h)
    to_x = [(other, grp, at(y, hh, c)) for hh in hs]
    to_y = [(side, grp, at(yu, h, c)), (side, grp, at(yd, h, c))]
    to_sib = (side, grp, at(y, h, 1 - c))
    to_z = [(side, gu, blk), (side, gd, blk)]

    barrier = pltpu.get_barrier_semaphore()
    partners = [*to_x, *to_y, to_sib, *to_z]
    for target in partners:
        pl.semaphore_signal(barrier, inc=1, device_id=target, device_id_type=MESH)

    small = [
        pltpu.make_async_copy(src, dst, in_sem.at[i])
        for i, (src, dst) in enumerate((
            (exps_hbm, exps_ref), (deg_hbm, deg_ref), (codes_hbm, codes_ref), (index_hbm, index_ref)))
    ]
    for copy in small:
        copy.start()
    adj_copies = []
    per = SLOTS // ADJ_PIECES
    for piece in range(ADJ_PIECES):
        cut = pl.ds(piece * per, per)
        copy = pltpu.make_async_copy(adj_ref.at[cut], a_ref.at[cut], adj_sem.at[piece])
        copy.start()
        adj_copies.append(copy)

    def inverse(tile):
        lanes = deg_ref[0:1, tile * TILE:(tile + 1) * TILE].astype(jnp.float32)
        return jnp.broadcast_to(lax.rsqrt(lanes), (TILE, TILE))

    for copy in small[:3]:
        copy.wait()
    for tile in range(TPS):
        power = jnp.exp2(jnp.full((TILE, TILE), exps_ref[0, tile], jnp.int32).astype(jnp.float32))
        rows = jnp.transpose(codes_ref[0, pl.ds(tile * TILE, TILE), :].astype(jnp.float32))
        rows = (rows * power * inverse(tile)).astype(jnp.bfloat16)
        for half in range(2):
            cut = rows[half * FEATS:(half + 1) * FEATS]
            if tile < PART:
                own_ref[half, tile] = cut
            else:
                t_ref[half, y, tile - PART] = cut

    pl.semaphore_wait(barrier, len(partners))

    sends = []

    def send(src, dst, ssem, rsem, target):
        copy = pltpu.make_async_remote_copy(
            src_ref=src, dst_ref=dst, send_sem=ssem, recv_sem=rsem,
            device_id=target, device_id_type=MESH,
        )
        copy.start()
        sends.append(copy)

    def wait_in(dst, rsem):
        pltpu.make_async_copy(dst, dst, rsem).wait()

    def a_rows(half, yy, hh, cc):
        return s_refs[half].at[pl.ds(at(yy, hh, cc) * TPS, PART)]

    def b_rows(half, yy, hh, cc):
        return s_refs[half].at[pl.ds(at(yy, hh, cc) * TPS + PART, PART)]

    for half in range(2):
        for i in range(2):
            send(own_ref.at[half], a_rows(half, y, h, c), xa_s.at[half, i], xa_r.at[half, i], to_x[i])
            send(t_ref.at[half, y], t_ref.at[half, y], t_s.at[half, i], t_r.at[half, i], to_y[i])
        for i in range(2):
            send(t_ref.at[half, y], b_rows(half, y, h, c), xb_s.at[half, 0, i], xb_r.at[half, 0, i], to_x[i])

    small[3].wait()
    sub = lax.broadcasted_iota(jnp.int32, (TILE, TILE), 0)
    lane = lax.broadcasted_iota(jnp.int32, (TILE, TILE), 1)
    lane_row = lax.broadcasted_iota(jnp.int32, (1, TILE), 1)
    cuts = range(SLOTS // TILE)

    def column(row):
        return jnp.transpose(jnp.broadcast_to(row, (TILE, TILE)))

    def down(mask, value=1):
        return jnp.sum(jnp.where(mask, value, 0), axis=0, keepdims=True)

    target = [index_ref[0, 0:1, j * TILE:(j + 1) * TILE] for j in cuts]
    source = [index_ref[0, 1:2, j * TILE:(j + 1) * TILE] for j in cuts]
    used = [q < NSRC for q in source]
    shift = (GROUPS + GROUPS // 2 - grp) * TPS
    key = [jnp.where(u, (t + shift) & (DST - 1), DST) for u, t in zip(used, target)]
    key_col = [column(t) for t in key]
    count = sum(down(k == lane) for k in key_col)
    padded = jnp.where(lane_row < DST, (count + 1) & ~1, 0)
    padded_col = column(padded)
    begin = down(sub < lane, padded_col)
    begin_col = column(begin)
    place_col, code_col = [], []
    for j in cuts:
        rank = down((key_col[j] == key[j]) & (sub < lane))
        for i in range(j):
            rank = rank + down(key_col[i] == key[j])
        place = down(sub < key[j], padded_col) + rank
        place_col.append(column(jnp.where(used[j], place, 8 * TILE)))
        code_col.append(((j * TILE + sub) * NSRC + column(source[j])) * 2)
    for r in range(4):
        spot = lane + r * TILE
        code = jnp.full((TILE, TILE), -1, jnp.int32)
        for j in cuts:
            code = jnp.where(place_col[j] == spot, code_col[j], code)
        code = jnp.max(code, axis=0, keepdims=True)
        first = down((begin_col == spot) & (padded_col > 0))
        tblv_ref[r:r + 1, :] = jnp.where(code < 0, SLOTS * NSRC * 2, code) + first
    tblv_ref[4:5, :] = jnp.where(padded > 0, ((begin + padded) >> 1) - 1, PAIRS)
    tbl_copy = pltpu.make_async_copy(tblv_ref, tbl_ref, tbl_sem)
    tbl_copy.start()
    a_ref[SLOTS] = jnp.zeros((TILE, TILE), jnp.bfloat16)
    for half in range(2):
        sum_ref[half, PAIRS] = jnp.zeros((FEATS, TILE), jnp.float32)

    def products(half, segment, total):
        first_pair, length, unroll = SEGMENTS[segment]

        def some(step, total):
            for j in range(unroll):
                pair = first_pair + step * unroll + j
                spot = pair * 2
                one = tbl_ref[spot >> 7, spot & (TILE - 1)]
                two = tbl_ref[spot >> 7, (spot & (TILE - 1)) + 1]
                left = jnp.concatenate(
                    [s_refs[half][(one >> 1) & (NSRC - 1)], s_refs[half][(two >> 1) & (NSRC - 1)]], axis=1)
                right = jnp.concatenate([a_ref[one >> 7], a_ref[two >> 7]], axis=1)
                value = lax.dot_general(
                    left, right, (((1,), (1,)), ((), ())), preferred_element_type=jnp.float32)
                keep = (1 - (one & 1)).astype(jnp.float32)
                total = value + total * keep
                sum_ref[half, pair] = total
            return total

        return lax.fori_loop(0, length // unroll, some, total)

    def summed(half, away, part):
        at_tile = (away + GROUPS // 2) % GROUPS * TPS + part * PART
        return [sum_ref[half, tbl_ref[4, at_tile + j]] for j in range(PART)]

    def ring(half, m, way):
        reach = 4 - (m + 1) // 2
        part = (m % 2) ^ way
        values = summed(half, reach if way == 0 else GROUPS - reach, part)
        if m >= 2:
            wait_in(ring_in.at[half, way, m - 2], ring_r.at[half, way, m - 2])
        for j in range(PART):
            value = values[j]
            if m >= 2:
                value = value + ring_in[half, way, m - 2, j].astype(jnp.float32)
            ring_out[half, way, m, j] = value.astype(jnp.bfloat16)
        send(ring_out.at[half, way, m], ring_in.at[half, way, m],
             ring_s.at[half, way, m], ring_r.at[half, way, m], to_z[way])

    def both(half, m):
        for way in range(2):
            ring(half, m, way)

    def final(half):
        for m in (5, 6):
            for way in range(2):
                wait_in(ring_in.at[half, way, m], ring_r.at[half, way, m])
        for part in range(2):
            values = summed(half, 0, part)
            for j in range(PART):
                value = values[j] + ring_in[half, part, 6, j].astype(jnp.float32)
                value = value + ring_in[half, 1 - part, 5, j].astype(jnp.float32)
                fin_ref[part * PART + j, pl.ds(half * FEATS, FEATS), :] = value

    ys = (y, yu, yd, yo)

    def hand(half, number, ref):
        send(ref, ref, sib_s.at[half, number], sib_r.at[half, number], to_sib)

    def sib_in(half):
        for number in range(16):
            k = number % 8
            rows = a_rows if number < 8 else b_rows
            wait_in(rows(half, ys[k // 2], hs[k % 2], 1 - c), sib_r.at[half, number])

    def level1(half):
        for i in range(2):
            frm = yd if i == 0 else yu
            wait_in(t_ref.at[half, frm], t_r.at[half, i])
            tile = t_ref.at[half, frm, i]
            send(tile, tile, tr_s.at[half, i], tr_r.at[half, i], to_y[i])
            for v in range(2):
                send(t_ref.at[half, frm], b_rows(half, frm, h, c),
                     xb_s.at[half, 2 - i, v], xb_r.at[half, 2 - i, v], to_x[v])
        for i in range(2):
            ref = a_rows(half, y, hs[i], c)
            wait_in(ref, xa_r.at[half, i])
            for v in range(2):
                send(ref, ref, ya_s.at[half, v, i], ya_r.at[half, v, i], to_y[v])
            hand(half, i, ref)
        for i in range(2):
            ref = b_rows(half, y, hs[i], c)
            wait_in(ref, xb_r.at[half, 0, i])
            hand(half, 8 + i, ref)

    def level2(half):
        for i in range(2):
            wait_in(t_ref.at[half, yo, i], tr_r.at[half, i])
        for i in range(2):
            send(t_ref.at[half, yo], b_rows(half, yo, h, c),
                 xb_s.at[half, 3, i], xb_r.at[half, 3, i], to_x[i])
        for i in range(2):
            for v in (i, 1 - i):
                frm = yd if v == 0 else yu
                ref = a_rows(half, frm, hs[i], c)
                wait_in(ref, ya_r.at[half, v, i])
                if i == v:
                    send(ref, ref, yr_s.at[half, i], yr_r.at[half, i], to_y[v])
                hand(half, (4 if v == 0 else 2) + i, ref)
        for n, frm in ((2, yd), (1, yu)):
            for i in range(2):
                ref = b_rows(half, frm, hs[i], c)
                wait_in(ref, xb_r.at[half, n, i])
                hand(half, 8 + 2 * n + i, ref)

    def level3(half):
        for i in range(2):
            ref = b_rows(half, yo, hs[i], c)
            wait_in(ref, xb_r.at[half, 3, i])
            hand(half, 14 + i, ref)
        for i in range(2):
            ref = a_rows(half, yo, hs[i], c)
            wait_in(ref, yr_r.at[half, i])
            hand(half, 6 + i, ref)

    level1(0)
    level1(1)
    level2(0)
    tbl_copy.wait()
    for copy in adj_copies:
        copy.wait()
    level2(1)
    level3(0)
    sib_in(0)
    nothing = jnp.zeros((FEATS, TILE), jnp.float32)
    total = products(0, 0, nothing)
    ring(0, 0, 0)
    total = products(0, 1, total)
    ring(0, 0, 1)
    level3(1)
    total = products(0, 2, total)
    both(0, 1)
    sib_in(1)
    total = products(1, 0, nothing)
    ring(1, 0, 0)
    both(0, 2)
    total = products(1, 1, total)
    ring(1, 0, 1)
    both(0, 3)
    total = products(1, 2, total)
    both(1, 1)
    both(0, 4)
    both(1, 2)
    both(0, 5)
    both(1, 3)
    both(0, 6)
    both(1, 4)
    both(1, 5)
    both(1, 6)
    final(0)
    final(1)
    for tile in range(TPS):
        value = fin_ref[tile] * inverse(tile)
        out_ref[0, pl.ds(tile * TILE, TILE), :] = jnp.transpose(value).astype(jnp.bfloat16)
    for copy in sends:
        copy.wait_send()


def shards(embed_codes, embed_exps, degrees, adjacency, block_index):
    dma = pltpu.SemaphoreType.DMA
    narrow = jnp.bfloat16
    sems = []
    for shape in ((2, 2), (2, 4, 2), (2, 2, 2), (2, 2), (2, 2), (2, 2), (2, 16), (2, 2, 7)):
        sems += [dma(shape), dma(shape)]
    return pl.pallas_call(
        kernel,
        out_shape=jax.ShapeDtypeStruct(embed_codes.shape, narrow),
        in_specs=[pl.BlockSpec(memory_space=pltpu.HBM)] * 5,
        out_specs=pl.BlockSpec(memory_space=pltpu.VMEM),
        scratch_shapes=[
            pltpu.VMEM((SLOTS + 1, TILE, TILE), narrow),
            pltpu.VMEM((NSRC, FEATS, TILE), narrow),
            pltpu.VMEM((NSRC, FEATS, TILE), narrow),
            pltpu.VMEM((2, NY, PART, FEATS, TILE), narrow),
            pltpu.VMEM((2, PART, FEATS, TILE), narrow),
            pltpu.VMEM((2, PAIRS + 1, FEATS, TILE), jnp.float32),
            pltpu.VMEM((TPS, TILE, TILE), jnp.float32),
            pltpu.VMEM((8, TILE), jnp.int32),
            pltpu.SMEM((8, TILE), jnp.int32),
            pltpu.VMEM(embed_codes.shape, embed_codes.dtype),
            pltpu.SMEM(embed_exps.shape, embed_exps.dtype),
            pltpu.VMEM(degrees.shape, degrees.dtype),
            pltpu.VMEM(block_index.shape, block_index.dtype),
            pltpu.VMEM((2, 2, 7, PART, FEATS, TILE), narrow),
            pltpu.VMEM((2, 2, 7, PART, FEATS, TILE), narrow),
            dma((4,)), dma((ADJ_PIECES,)), dma(()),
            *sems,
        ],
        compiler_params=pltpu.CompilerParams(
            collective_id=0, has_side_effects=True, vmem_limit_bytes=67_043_328
        ),
    )(embed_codes, embed_exps, degrees, adjacency.reshape(adjacency.shape[1:]), block_index)


def solution(mesh):
    placed = (
        P("side", ("grp", "blk"), None),
        P("side", ("grp", "blk")),
        P("side", ("grp", "blk")),
        P("side", ("grp", "blk"), None, None),
        P("side", None, ("grp", "blk")),
    )
    return jax.shard_map(
        shards,
        mesh=mesh,
        in_specs=placed,
        out_specs=P("side", ("grp", "blk"), None),
        check_vma=False,
    )
```

time: 50.5 us -> 47.8 us (0.947)
  Pallas kernels: 48.8 us -> 46.2 us
    pallas_call x1, Pallas kernels: 48.8 us -> 46.2 us  [shards(): pl.pallas_call(kernel, out_shape=jax.ShapeDtypeStruct(embed_codes.shape,...]
where the time goes in v3:
time: 47.8 us
  Pallas kernels  46.2 us (97%)
  local copies, waits for them, and re-layouts  1.57 us (3%)
    pallas_call x1, Pallas kernels, shards(): pl.pallas_call(kernel, out_shape=jax.ShapeDtypeStruct(embed_codes.shape,...  46.2 us
    unnamed x1, local copies, waits for them, and re-layouts  1.57 us

profile of v3, /device:TPU:1, one launch (start us, length us, event | category | flops | bytes accessed | tf_op | source)
XLA Modules:
  0.0 47.8 jit_solution(519547674921885636)
XLA Ops:
  0.0 46.2 %shard_map.55 = bf16[1,512,128]{2,1,0:T(8,128)(2,1)} custom-call(bf16[1,512,128]{2,1,0:T(8,128)(2,1)} %codes_hbm.1, s32[1,4]{1,0:T(1,128)} %exps_hbm.1, s32[1,512]{1,0:T(1,128)} %deg_hbm.1, bf16[384,128,128]{2,1,0:T(8,128)(2,1)} %bitcast.1, s32[1,2,384]{2,1,0:T(2,128)} %index_hbm.1), custom_call_target="tpu_custom_call" | custom-call | tf_op jit(solution)/shard_map/pallas_call | solution.py:325
  46.2 1.6 %copy.7 = bf16[1,512,128]{2,1,0:T(8,128)(2,1)} copy(bf16[1,512,128]{2,1,0:T(8,128)(2,1)} %shard_map.55) | data formatting | bytes 262144

commit v4 on v2

v4 whole, which is shorter than its diff:
```python
import jax
import jax.numpy as jnp
from jax import lax
from jax.experimental import pallas as pl
from jax.experimental.pallas import tpu as pltpu
from jax.sharding import PartitionSpec as P

MESH = pl.DeviceIdType.MESH
TILE = 128
TPS = 4
ROWS = TILE * TPS
PART = TPS // 2
NY, NH, NC = 4, 2, 2
GROUPS = 8
DST = 32
SLOTS = 384
ADJ_PIECES = 8
PAIRS = (SLOTS + DST) // 2
NSRC = 64
SEGMENTS = (0, 32, 64, 96, 128, 208)


def kernel(
    codes_hbm, exps_hbm, deg_hbm, adj_ref, index_hbm, out_ref,
    a_ref, s_ref, t_ref, own_ref, sum_ref, inv_ref, tblv_ref, tbl_ref,
    codes_ref, exps_ref, deg_ref, index_ref,
    ring_out, ring_in,
    in_sem, adj_sem, tbl_sem,
    xa_s, xa_r, xb_s, xb_r, xc_s, xc_r, ya_s, ya_r, yr_s, yr_r, t_s, t_r, tr_s, tr_r,
    sib_s, sib_r, ring_s, ring_r,
):
    side = lax.axis_index("side")
    grp = lax.axis_index("grp")
    blk = lax.axis_index("blk")
    y, h, c = blk // (NH * NC), (blk // NC) % NH, blk % NC
    other = 1 - side

    def at(yy, hh, cc):
        return (yy * NH + hh) * NC + cc

    yu, yd, yo = (y + 1) % NY, (y + NY - 1) % NY, (y + 2) % NY
    gu, gd = (grp + 1) % GROUPS, (grp + GROUPS - 1) % GROUPS
    hs = (h, 1 - h)
    to_x = [(other, grp, at(y, hh, c)) for hh in hs]
    to_y = [(side, grp, at(yu, h, c)), (side, grp, at(yd, h, c))]
    to_sib = (side, grp, at(y, h, 1 - c))
    to_z = [(side, gu, blk), (side, gd, blk)]

    barrier = pltpu.get_barrier_semaphore()
    partners = [*to_x, *to_y, to_sib, *to_z]
    for target in partners:
        pl.semaphore_signal(barrier, inc=1, device_id=target, device_id_type=MESH)

    small = [
        pltpu.make_async_copy(src, dst, in_sem.at[i])
        for i, (src, dst) in enumerate((
            (exps_hbm, exps_ref), (deg_hbm, deg_ref), (codes_hbm, codes_ref), (index_hbm, index_ref)))
    ]
    for copy in small:
        copy.start()
    adj_copies = []
    per = SLOTS // ADJ_PIECES
    for piece in range(ADJ_PIECES):
        cut = pl.ds(piece * per, per)
        copy = pltpu.make_async_copy(adj_ref.at[cut], a_ref.at[cut], adj_sem.at[piece])
        copy.start()
        adj_copies.append(copy)

    def column(row):
        return jnp.transpose(jnp.broadcast_to(row, (TILE, TILE)))

    for copy in small[:3]:
        copy.wait()
    for tile in range(TPS):
        lanes = deg_ref[0:1, tile * TILE:(tile + 1) * TILE].astype(jnp.float32)
        inverse = column(lax.rsqrt(lanes))
        inv_ref[pl.ds(tile * TILE, TILE), :] = inverse
        power = jnp.exp2(jnp.full((TILE, TILE), exps_ref[0, tile], jnp.int32).astype(jnp.float32))
        rows = codes_ref[0, pl.ds(tile * TILE, TILE), :].astype(jnp.float32)
        rows = (rows * power * inverse).astype(jnp.bfloat16)
        if tile < TPS // 2:
            own_ref[tile] = rows
        else:
            t_ref[y, tile - TPS // 2] = rows

    pl.semaphore_wait(barrier, len(partners))

    sends = []

    def send(src, dst, ssem, rsem, target):
        copy = pltpu.make_async_remote_copy(
            src_ref=src, dst_ref=dst, send_sem=ssem, recv_sem=rsem,
            device_id=target, device_id_type=MESH,
        )
        copy.start()
        sends.append(copy)

    def wait_in(dst, rsem):
        pltpu.make_async_copy(dst, dst, rsem).wait()

    def tiles(yy, hh, cc, first, count):
        return s_ref.at[pl.ds(at(yy, hh, cc) * TPS + first, count)]

    for j in range(PART):
        for i in range(2):
            send(own_ref.at[j], s_ref.at[at(y, h, c) * TPS + j], xa_s.at[j, i], xa_r.at[j, i], to_x[i])
            k = i ^ j
            send(t_ref.at[y, k], t_ref.at[y, k], t_s.at[i, k], t_r.at[i, k], to_y[i])
    for i in range(2):
        send(t_ref.at[y], tiles(y, h, c, PART, PART), xb_s.at[0, i], xb_r.at[0, i], to_x[i])

    small[3].wait()
    sub = lax.broadcasted_iota(jnp.int32, (TILE, TILE), 0)
    lane = lax.broadcasted_iota(jnp.int32, (TILE, TILE), 1)
    lane_row = lax.broadcasted_iota(jnp.int32, (1, TILE), 1)
    cuts = range(SLOTS // TILE)

    def down(mask, value=1):
        return jnp.sum(jnp.where(mask, value, 0), axis=0, keepdims=True)

    target = [index_ref[0, 0:1, j * TILE:(j + 1) * TILE] for j in cuts]
    source = [index_ref[0, 1:2, j * TILE:(j + 1) * TILE] for j in cuts]
    used = [q < NSRC for q in source]
    shift = (GROUPS + GROUPS // 2 - grp) * TPS

    def order(t):
        group = (t + shift) & (DST - TPS)
        return group + ((t & 1) << 1) + ((t >> 1) & 1)

    key = [jnp.where(u, order(t), DST) for u, t in zip(used, target)]
    key_col = [column(t) for t in key]
    count = sum(down(k == lane) for k in key_col)
    padded = jnp.where(lane_row < DST, (count + 1) & ~1, 0)
    padded_col = column(padded)
    begin = down(sub < lane, padded_col)
    begin_col = column(begin)
    place_col, code_col = [], []
    for j in cuts:
        rank = down((key_col[j] == key[j]) & (sub < lane))
        for i in range(j):
            rank = rank + down(key_col[i] == key[j])
        place = down(sub < key[j], padded_col) + rank
        place_col.append(column(jnp.where(used[j], place, 8 * TILE)))
        code_col.append(((j * TILE + sub) * NSRC + column(source[j])) * 2)
    for r in range(4):
        spot = lane + r * TILE
        code = jnp.full((TILE, TILE), -1, jnp.int32)
        for j in cuts:
            code = jnp.where(place_col[j] == spot, code_col[j], code)
        code = jnp.max(code, axis=0, keepdims=True)
        first = down((begin_col == spot) & (padded_col > 0))
        tblv_ref[r:r + 1, :] = jnp.where(code < 0, SLOTS * NSRC * 2, code) + first
    tblv_ref[4:5, :] = jnp.where(padded > 0, ((begin + padded) >> 1) - 1, PAIRS)
    tbl_copy = pltpu.make_async_copy(tblv_ref, tbl_ref, tbl_sem)
    tbl_copy.start()
    a_ref[SLOTS] = jnp.zeros((TILE, TILE), jnp.bfloat16)
    sum_ref[PAIRS] = jnp.zeros((TILE, TILE), jnp.float32)

    def products(segment, total):
        for pair in range(SEGMENTS[segment], SEGMENTS[segment + 1]):
            row, spot = pair // (TILE // 2), pair % (TILE // 2) * 2
            one, two = tbl_ref[row, spot], tbl_ref[row, spot + 1]
            left = jnp.concatenate([a_ref[one >> 7], a_ref[two >> 7]], axis=1)
            right = jnp.concatenate(
                [s_ref[(one >> 1) & (NSRC - 1)], s_ref[(two >> 1) & (NSRC - 1)]], axis=0)
            value = jnp.dot(left, right, preferred_element_type=jnp.float32)
            keep = (1 - (one & 1)).astype(jnp.float32)
            total = value + total * keep
            sum_ref[pair] = total
        return total

    def summed(away, part, j):
        return sum_ref[tbl_ref[4, (away + GROUPS // 2) % GROUPS * TPS + j * PART + part]]

    def ring(m, way, j):
        reach = 4 - (m + 1) // 2
        value = summed(reach if way == 0 else GROUPS - reach, (m % 2) ^ way, j)
        if m >= 2:
            wait_in(ring_in.at[way, m - 2, j], ring_r.at[way, m - 2, j])
            value = value + ring_in[way, m - 2, j].astype(jnp.float32)
        ring_out[way, m, j] = value.astype(jnp.bfloat16)
        send(ring_out.at[way, m, j], ring_in.at[way, m, j],
             ring_s.at[way, m, j], ring_r.at[way, m, j], to_z[way])

    expected = []

    def hand(yy, i, first, count):
        number = len(expected)
        ref = tiles(yy, hs[i], c, first, count)
        send(ref, ref, sib_s.at[number], sib_r.at[number], to_sib)
        expected.append(tiles(yy, hs[i], 1 - c, first, count))

    def wait_tiles(yy, i, first, count, rsem):
        ref = tiles(yy, hs[i], c, first, count)
        wait_in(ref, rsem)
        return ref

    near = (yd, yu)
    for i in range(2):
        tile = t_ref.at[near[i], i]
        wait_in(tile, t_r.at[i, i])
        send(tile, tile, tr_s.at[i], tr_r.at[i], to_y[i])

    def pass_on(j, i, v):
        ref = tiles(y, hs[i], c, j, 1)
        send(ref, ref, ya_s.at[v, i, j], ya_r.at[v, i, j], to_y[v])

    for i in range(2):
        wait_tiles(y, i, 0, 1, xa_r.at[0, i])
        pass_on(0, i, i)
    for i in range(2):
        wait_in(t_ref.at[near[i], 1 - i], t_r.at[i, 1 - i])
        for v in range(2):
            send(t_ref.at[near[i]], tiles(near[i], h, c, PART, PART),
                 xb_s.at[2 - i, v], xb_r.at[2 - i, v], to_x[v])
    for i in range(2):
        wait_tiles(y, i, 1, 1, xa_r.at[1, i])
        pass_on(1, i, i)
    for j in range(PART):
        for i in range(2):
            pass_on(j, i, 1 - i)
    for i in range(2):
        hand(y, i, 0, PART)
    for i in range(2):
        wait_tiles(y, i, PART, PART, xb_r.at[0, i])
        hand(y, i, PART, PART)
    for i in range(2):
        wait_in(t_ref.at[yo, i], tr_r.at[i])
        for v in range(2):
            send(t_ref.at[yo, i], s_ref.at[at(yo, h, c) * TPS + PART + i],
                 xc_s.at[i, v], xc_r.at[i, v], to_x[v])
    for j in range(PART):
        for i in range(2):
            ref = wait_tiles(near[i], i, j, 1, ya_r.at[i, i, j])
            send(ref, ref, yr_s.at[i, j], yr_r.at[i, j], to_y[i])
    for i in range(2):
        hand(near[i], i, 0, PART)
    for i in range(2):
        for v in range(2):
            wait_tiles(near[i], v, PART, PART, xb_r.at[2 - i, v])
            hand(near[i], v, PART, PART)
    for i in range(2):
        for j in range(PART):
            wait_tiles(near[i], 1 - i, j, 1, ya_r.at[i, 1 - i, j])
        hand(near[i], 1 - i, 0, PART)
    for j in range(PART):
        for i in range(2):
            wait_tiles(yo, i, PART + j, 1, xc_r.at[j, i])
            hand(yo, i, PART + j, 1)
        for i in range(2):
            wait_tiles(yo, i, j, 1, yr_r.at[i, j])
            hand(yo, i, j, 1)
    tbl_copy.wait()
    for copy in adj_copies:
        copy.wait()
    for number, ref in enumerate(expected):
        wait_in(ref, sib_r.at[number])

    total = jnp.zeros((TILE, TILE), jnp.float32)
    for segment in range(TPS):
        total = products(segment, total)
        ring(0, segment % 2, segment // 2)
    products(TPS, total)
    for m in range(1, 7):
        for j in range(PART):
            for way in range(2):
                ring(m, way, j)
    for j in range(PART):
        for m, way in ((5, 0), (5, 1), (6, 0), (6, 1)):
            wait_in(ring_in.at[way, m, j], ring_r.at[way, m, j])
        for part in range(2):
            value = summed(0, part, j) + ring_in[part, 6, j].astype(jnp.float32)
            value = value + ring_in[1 - part, 5, j].astype(jnp.float32)
            cut = pl.ds((part * PART + j) * TILE, TILE)
            out_ref[0, cut, :] = (value * inv_ref[cut, :]).astype(jnp.bfloat16)
    for copy in sends:
        copy.wait_send()


def shards(embed_codes, embed_exps, degrees, adjacency, block_index):
    width = embed_codes.shape[2]
    dma = pltpu.SemaphoreType.DMA
    vmem = pl.BlockSpec(memory_space=pltpu.VMEM)
    sems = []
    for shape in ((2, 2), (3, 2), (2, 2), (2, 2, 2), (2, 2), (2, 2), (2,), (20,), (2, 7, PART)):
        sems += [dma(shape), dma(shape)]
    return pl.pallas_call(
        kernel,
        out_shape=jax.ShapeDtypeStruct(embed_codes.shape, jnp.bfloat16),
        in_specs=[pl.BlockSpec(memory_space=pltpu.HBM)] * 5,
        out_specs=vmem,
        scratch_shapes=[
            pltpu.VMEM((SLOTS + 1, TILE, TILE), jnp.bfloat16),
            pltpu.VMEM((NSRC, TILE, width), jnp.bfloat16),
            pltpu.VMEM((NY, TPS // 2, TILE, width), jnp.bfloat16),
            pltpu.VMEM((TPS // 2, TILE, width), jnp.bfloat16),
            pltpu.VMEM((PAIRS + 1, TILE, width), jnp.float32),
            pltpu.VMEM((ROWS, width), jnp.float32),
            pltpu.VMEM((8, TILE), jnp.int32),
            pltpu.SMEM((8, TILE), jnp.int32),
            pltpu.VMEM(embed_codes.shape, embed_codes.dtype),
            pltpu.SMEM(embed_exps.shape, embed_exps.dtype),
            pltpu.VMEM(degrees.shape, degrees.dtype),
            pltpu.VMEM(block_index.shape, block_index.dtype),
            pltpu.VMEM((2, 7, PART, TILE, width), jnp.bfloat16),
            pltpu.VMEM((2, 7, PART, TILE, width), jnp.bfloat16),
            dma((4,)), dma((ADJ_PIECES,)), dma(()),
            *sems,
        ],
        compiler_params=pltpu.CompilerParams(
            collective_id=0, has_side_effects=True, vmem_limit_bytes=67_043_328
        ),
    )(embed_codes, embed_exps, degrees, adjacency.reshape(adjacency.shape[1:]), block_index)


def solution(mesh):
    placed = (
        P("side", ("grp", "blk"), None),
        P("side", ("grp", "blk")),
        P("side", ("grp", "blk")),
        P("side", ("grp", "blk"), None, None),
        P("side", None, ("grp", "blk")),
    )
    return jax.shard_map(
        shards,
        mesh=mesh,
        in_specs=placed,
        out_specs=P("side", ("grp", "blk"), None),
        check_vma=False,
    )
```

time: 50.5 us -> 43.1 us (0.85)
  Pallas kernels: 48.8 us -> 41.4 us
    pallas_call x1, Pallas kernels: 48.8 us -> 41.4 us  [shards(): pl.pallas_call(kernel, out_shape=jax.ShapeDtypeStruct(embed_codes.shape,...]
where the time goes in v4:
time: 43.1 us; the launch traced here: 43 us
  Pallas kernels  41.4 us (96%)
  local copies, waits for them, and re-layouts  1.57 us (4%)
    pallas_call x1, Pallas kernels, shards(): pl.pallas_call(kernel, out_shape=jax.ShapeDtypeStruct(embed_codes.shape,...  41.4 us
    unnamed x1, local copies, waits for them, and re-layouts  1.57 us

profile of v4, /device:TPU:1, one launch (start us, length us, event | category | flops | bytes accessed | tf_op | source)
XLA Modules:
  0.0 43.0 jit_solution(16594851070378435977)
XLA Ops:
  0.0 41.4 %shard_map.55 = bf16[1,512,128]{2,1,0:T(8,128)(2,1)} custom-call(bf16[1,512,128]{2,1,0:T(8,128)(2,1)} %codes_hbm.1, s32[1,4]{1,0:T(1,128)} %exps_hbm.1, s32[1,512]{1,0:T(1,128)} %deg_hbm.1, bf16[384,128,128]{2,1,0:T(8,128)(2,1)} %bitcast.1, s32[1,2,384]{2,1,0:T(2,128)} %index_hbm.1), custom_call_target="tpu_custom_call" | custom-call | tf_op jit(solution)/shard_map/pallas_call | solution.py:287
  41.4 1.6 %copy.7 = bf16[1,512,128]{2,1,0:T(8,128)(2,1)} copy(bf16[1,512,128]{2,1,0:T(8,128)(2,1)} %shard_map.55) | data formatting | bytes 262144

commit v5 on v4

--- a/solution.py
+++ b/solution.py
@@ -14,10 +14,10 @@
 GROUPS = 8
 DST = 32
 SLOTS = 384
-ADJ_PIECES = 8
+ADJ_PIECES = 2
 PAIRS = (SLOTS + DST) // 2
 NSRC = 64
-SEGMENTS = (0, 32, 64, 96, 128, 208)
+SEGMENTS = (0, 32, 64, 96, 128, 160, 192, 208)
 
 
 def kernel(
@@ -45,11 +45,7 @@
     to_y = [(side, grp, at(yu, h, c)), (side, grp, at(yd, h, c))]
     to_sib = (side, grp, at(y, h, 1 - c))
     to_z = [(side, gu, blk), (side, gd, blk)]
-
-    barrier = pltpu.get_barrier_semaphore()
-    partners = [*to_x, *to_y, to_sib, *to_z]
-    for target in partners:
-        pl.semaphore_signal(barrier, inc=1, device_id=target, device_id_type=MESH)
+    to_z2 = [(side, (grp + 2) % GROUPS, blk), (side, (grp + GROUPS - 2) % GROUPS, blk)]
 
     small = [
         pltpu.make_async_copy(src, dst, in_sem.at[i])
@@ -58,13 +54,10 @@
     ]
     for copy in small:
         copy.start()
-    adj_copies = []
-    per = SLOTS // ADJ_PIECES
-    for piece in range(ADJ_PIECES):
-        cut = pl.ds(piece * per, per)
-        copy = pltpu.make_async_copy(adj_ref.at[cut], a_ref.at[cut], adj_sem.at[piece])
-        copy.start()
-        adj_copies.append(copy)
+    barrier = pltpu.get_barrier_semaphore()
+    partners = [*to_z2, *to_z, *to_x, *to_y, to_sib]
+    for target in partners:
+        pl.semaphore_signal(barrier, inc=1, device_id=target, device_id_type=MESH)
 
     def column(row):
         return jnp.transpose(jnp.broadcast_to(row, (TILE, TILE)))
@@ -95,6 +88,10 @@
         copy.start()
         sends.append(copy)
 
+    def settle(keep=0):
+        while len(sends) > keep:
+            sends.pop(0).wait_send()
+
     def wait_in(dst, rsem):
         pltpu.make_async_copy(dst, dst, rsem).wait()
 
@@ -108,6 +105,14 @@
             send(t_ref.at[y, k], t_ref.at[y, k], t_s.at[i, k], t_r.at[i, k], to_y[i])
     for i in range(2):
         send(t_ref.at[y], tiles(y, h, c, PART, PART), xb_s.at[0, i], xb_r.at[0, i], to_x[i])
+
+    adj_copies = []
+    per = SLOTS // ADJ_PIECES
+    for piece in range(ADJ_PIECES):
+        cut = pl.ds(piece * per, per)
+        copy = pltpu.make_async_copy(adj_ref.at[cut], a_ref.at[cut], adj_sem.at[piece])
+        copy.start()
+        adj_copies.append(copy)
 
     small[3].wait()
     sub = lax.broadcasted_iota(jnp.int32, (TILE, TILE), 0)
@@ -124,8 +129,11 @@
     shift = (GROUPS + GROUPS // 2 - grp) * TPS
 
     def order(t):
-        group = (t + shift) & (DST - TPS)
-        return group + ((t & 1) << 1) + ((t >> 1) & 1)
+        group, tile = ((t + shift) & (DST - 1)) >> 2, t & 3
+        turn = ((tile & 1) << 1) + (tile >> 1)
+        near = jnp.where(group == 1, TPS + 2 * turn, TPS + 1 + 2 * (turn ^ 1))
+        rest = 3 * TPS + (group - 2) * TPS + tile
+        return jnp.where(group == 0, turn, jnp.where((group == 1) | (group == 7), near, rest))
 
     key = [jnp.where(u, order(t), DST) for u, t in zip(used, target)]
     key_col = [column(t) for t in key]
@@ -170,17 +178,26 @@
         return total
 
     def summed(away, part, j):
-        return sum_ref[tbl_ref[4, (away + GROUPS // 2) % GROUPS * TPS + j * PART + part]]
+        group, turn = (away + GROUPS // 2) % GROUPS, j * PART + part
+        if group == 0:
+            spot = turn
+        elif group == 1:
+            spot = TPS + 2 * turn
+        elif group == 7:
+            spot = TPS + 1 + 2 * (turn ^ 1)
+        else:
+            spot = 3 * TPS + (group - 2) * TPS + part * PART + j
+        return sum_ref[tbl_ref[4, spot]]
 
     def ring(m, way, j):
         reach = 4 - (m + 1) // 2
         value = summed(reach if way == 0 else GROUPS - reach, (m % 2) ^ way, j)
-        if m >= 2:
-            wait_in(ring_in.at[way, m - 2, j], ring_r.at[way, m - 2, j])
-            value = value + ring_in[way, m - 2, j].astype(jnp.float32)
+        for n in {3: (1,), 4: (0, 2), 5: (3,), 6: (4,)}.get(m, ()):
+            wait_in(ring_in.at[way, n, j], ring_r.at[way, n, j])
+            value = value + ring_in[way, n, j].astype(jnp.float32)
         ring_out[way, m, j] = value.astype(jnp.bfloat16)
         send(ring_out.at[way, m, j], ring_in.at[way, m, j],
-             ring_s.at[way, m, j], ring_r.at[way, m, j], to_z[way])
+             ring_s.at[way, m, j], ring_r.at[way, m, j], to_z2[way] if m == 0 else to_z[way])
 
     expected = []
 
@@ -257,14 +274,17 @@
         wait_in(ref, sib_r.at[number])
 
     total = jnp.zeros((TILE, TILE), jnp.float32)
-    for segment in range(TPS):
+    early = ((0, 0, 0), (0, 1, 0), (0, 0, 1), (0, 1, 1), (1, 1, 0), (1, 0, 0))
+    for segment, piece in enumerate(early):
         total = products(segment, total)
-        ring(0, segment % 2, segment // 2)
-    products(TPS, total)
-    for m in range(1, 7):
-        for j in range(PART):
-            for way in range(2):
-                ring(m, way, j)
+        ring(*piece)
+    products(len(early), total)
+    for m, j in ((2, 0), (1, 1), (2, 1)):
+        for way in range(2):
+            ring(m, way, j)
+    for m, j in ((3, 0), (4, 0), (3, 1), (4, 1), (5, 0), (6, 0), (5, 1), (6, 1)):
+        for way in range(2):
+            ring(m, way, j)
     for j in range(PART):
         for m, way in ((5, 0), (5, 1), (6, 0), (6, 1)):
             wait_in(ring_in.at[way, m, j], ring_r.at[way, m, j])
@@ -273,8 +293,7 @@
             value = value + ring_in[1 - part, 5, j].astype(jnp.float32)
             cut = pl.ds((part * PART + j) * TILE, TILE)
             out_ref[0, cut, :] = (value * inv_ref[cut, :]).astype(jnp.bfloat16)
-    for copy in sends:
-        copy.wait_send()
+    settle()
 
 
 def shards(embed_codes, embed_exps, degrees, adjacency, block_index):

time: 43.1 us -> 40.3 us (0.935)
  Pallas kernels: 41.4 us -> 38.6 us
    pallas_call x1, Pallas kernels: 41.4 us -> 38.6 us  [shards(): pl.pallas_call(kernel, out_shape=jax.ShapeDtypeStruct(embed_codes.shape,...]
where the time goes in v5:
time: 40.3 us; the launch traced here: 40.2 us
  Pallas kernels  38.6 us (96%)
  local copies, waits for them, and re-layouts  1.57 us (4%)
    pallas_call x1, Pallas kernels, shards(): pl.pallas_call(kernel, out_shape=jax.ShapeDtypeStruct(embed_codes.shape,...  38.6 us
    unnamed x1, local copies, waits for them, and re-layouts  1.57 us

profile of v5, /device:TPU:1, one launch (start us, length us, event | category | flops | bytes accessed | tf_op | source)
XLA Modules:
  0.0 40.2 jit_solution(10703390090528789471)
XLA Ops:
  0.0 38.6 %shard_map.55 = bf16[1,512,128]{2,1,0:T(8,128)(2,1)} custom-call(bf16[1,512,128]{2,1,0:T(8,128)(2,1)} %codes_hbm.1, s32[1,4]{1,0:T(1,128)} %exps_hbm.1, s32[1,512]{1,0:T(1,128)} %deg_hbm.1, bf16[384,128,128]{2,1,0:T(8,128)(2,1)} %bitcast.1, s32[1,2,384]{2,1,0:T(2,128)} %index_hbm.1), custom_call_target="tpu_custom_call" | custom-call | tf_op jit(solution)/shard_map/pallas_call | solution.py:306
  38.6 1.6 %copy.7 = bf16[1,512,128]{2,1,0:T(8,128)(2,1)} copy(bf16[1,512,128]{2,1,0:T(8,128)(2,1)} %shard_map.55) | data formatting | bytes 262144

commit v6 on v5

--- a/solution.py
+++ b/solution.py
@@ -104,7 +104,7 @@
             k = i ^ j
             send(t_ref.at[y, k], t_ref.at[y, k], t_s.at[i, k], t_r.at[i, k], to_y[i])
     for i in range(2):
-        send(t_ref.at[y], tiles(y, h, c, PART, PART), xb_s.at[0, i], xb_r.at[0, i], to_x[i])
+        send(t_ref.at[y], tiles(y, h, c, PART, PART), xb_s.at[0, i, 0], xb_r.at[0, i, 0], to_x[i])
 
     adj_copies = []
     per = SLOTS // ADJ_PIECES
@@ -212,11 +212,18 @@
         wait_in(ref, rsem)
         return ref
 
+    def over(i, turn):
+        k = i ^ turn
+        for v in range(2):
+            send(t_ref.at[near[i], k], s_ref.at[at(near[i], h, c) * TPS + PART + k],
+                 xb_s.at[2 - i, v, turn], xb_r.at[2 - i, v, turn], to_x[v])
+
     near = (yd, yu)
     for i in range(2):
         tile = t_ref.at[near[i], i]
         wait_in(tile, t_r.at[i, i])
         send(tile, tile, tr_s.at[i], tr_r.at[i], to_y[i])
+        over(i, 0)
 
     def pass_on(j, i, v):
         ref = tiles(y, hs[i], c, j, 1)
@@ -227,9 +234,7 @@
         pass_on(0, i, i)
     for i in range(2):
         wait_in(t_ref.at[near[i], 1 - i], t_r.at[i, 1 - i])
-        for v in range(2):
-            send(t_ref.at[near[i]], tiles(near[i], h, c, PART, PART),
-                 xb_s.at[2 - i, v], xb_r.at[2 - i, v], to_x[v])
+        over(i, 1)
     for i in range(2):
         wait_tiles(y, i, 1, 1, xa_r.at[1, i])
         pass_on(1, i, i)
@@ -239,7 +244,7 @@
     for i in range(2):
         hand(y, i, 0, PART)
     for i in range(2):
-        wait_tiles(y, i, PART, PART, xb_r.at[0, i])
+        wait_tiles(y, i, PART, PART, xb_r.at[0, i, 0])
         hand(y, i, PART, PART)
     for i in range(2):
         wait_in(t_ref.at[yo, i], tr_r.at[i])
@@ -254,7 +259,8 @@
         hand(near[i], i, 0, PART)
     for i in range(2):
         for v in range(2):
-            wait_tiles(near[i], v, PART, PART, xb_r.at[2 - i, v])
+            for turn in range(2):
+                wait_tiles(near[i], v, PART + (i ^ turn), 1, xb_r.at[2 - i, v, turn])
             hand(near[i], v, PART, PART)
     for i in range(2):
         for j in range(PART):
@@ -301,7 +307,7 @@
     dma = pltpu.SemaphoreType.DMA
     vmem = pl.BlockSpec(memory_space=pltpu.VMEM)
     sems = []
-    for shape in ((2, 2), (3, 2), (2, 2), (2, 2, 2), (2, 2), (2, 2), (2,), (20,), (2, 7, PART)):
+    for shape in ((2, 2), (3, 2, 2), (2, 2), (2, 2, 2), (2, 2), (2, 2), (2,), (20,), (2, 7, PART)):
         sems += [dma(shape), dma(shape)]
     return pl.pallas_call(
         kernel,

time: 40.3 us -> 40.5 us (level)
  no operation moved by 1% of the time
where the time goes in v6:
time: 40.5 us; the launch traced here: 40.4 us
  Pallas kernels  38.8 us (96%)
  local copies, waits for them, and re-layouts  1.57 us (4%)
    pallas_call x1, Pallas kernels, shards(): pl.pallas_call(kernel, out_shape=jax.ShapeDtypeStruct(embed_codes.shape,...  38.8 us
    unnamed x1, local copies, waits for them, and re-layouts  1.57 us

profile of v6, /device:TPU:1, one launch (start us, length us, event | category | flops | bytes accessed | tf_op | source)
XLA Modules:
  0.0 40.4 jit_solution(9645913809112064486)
XLA Ops:
  0.0 38.8 %shard_map.55 = bf16[1,512,128]{2,1,0:T(8,128)(2,1)} custom-call(bf16[1,512,128]{2,1,0:T(8,128)(2,1)} %codes_hbm.1, s32[1,4]{1,0:T(1,128)} %exps_hbm.1, s32[1,512]{1,0:T(1,128)} %deg_hbm.1, bf16[384,128,128]{2,1,0:T(8,128)(2,1)} %bitcast.1, s32[1,2,384]{2,1,0:T(2,128)} %index_hbm.1), custom_call_target="tpu_custom_call" | custom-call | tf_op jit(solution)/shard_map/pallas_call | solution.py:312
  38.8 1.6 %copy.7 = bf16[1,512,128]{2,1,0:T(8,128)(2,1)} copy(bf16[1,512,128]{2,1,0:T(8,128)(2,1)} %shard_map.55) | data formatting | bytes 262144
